TPU v7x, 32 devices: a whole 2x2x4 slice. The times are simulated.
32 devices in a mesh: tm: 16 (over z, x, core), chan: 2 (over y).
Axes of the slice: x: 2, y: 2, z: 4, core: 2. Of those that a mesh axis runs over, the one named last changes fastest.
Arguments:
- series: float32 [64, 8192], P('chan', 'tm'), may hold values from -200 to 200
- tail: float32 [64, 127], P('chan'), may hold values from -200 to 200
- excl: int32 [1], replicated, may hold values from 32 to 128
Outputs:
- profile: float32 [8192], P('tm')
All inputs are finite; a program needn't handle non-finite values.
Results may differ from a plain program's by a relative error of at most 0.0003.
Values may be sent and summed in bfloat16 or wider, within the bound.
No kernel may reach another device: no remote copies, remote signals or barrier semaphores. Data moves between devices by JAX's collectives and lax.ppermute only.
A program may use at most 128 MiB of HBM per device.

v0:
```python
import math
import jax
import jax.numpy as jnp
from jax import lax
from jax.sharding import PartitionSpec as P

C = 64
EPSILON = 1e-05
CEILING = 4.0


def from_behind(shard, axis, by):
    length = lax.axis_size(axis)
    pairs = [(i, i + by) for i in range(length) if 0 <= i + by < length]
    return lax.ppermute(shard, axis, pairs)


def normalize(extended, count, length, channels):
    starts = (
        jnp.arange(length, dtype=jnp.int32)[:, None] + jnp.arange(count, dtype=jnp.int32)[None, :]
    )
    windows = extended[:, starts]
    center = jnp.mean(windows, axis=1, keepdims=True)
    shifted = windows - center
    spread = jnp.mean(shifted * shifted, axis=1, keepdims=True)
    factor = lax.rsqrt(spread + EPSILON) * (1.0 / math.sqrt(length * channels))
    return (shifted * factor).astype(jnp.bfloat16)


def correlate(left, right):
    return lax.dot_general(
        left, right, (((0, 1), (0, 1)), ((), ())), preferred_element_type=jnp.float32
    )


def on_device(series, tail, excl):
    count = series.shape[1]
    width = tail.shape[1]
    length = width + 1
    blocks = lax.axis_size("tm")
    block_index = lax.axis_index("tm")
    head = from_behind(series[:, :width], "tm", -1)
    head = jnp.where(block_index == blocks - 1, tail, head)
    extended = jnp.concatenate([series, head], axis=1)
    query = normalize(extended, count, length, C)
    nearby = from_behind(query, "tm", -1)
    faraway = from_behind(query, "tm", -2)
    limit = excl[0]

    def scored(total, row_pos, offset):
        columns = (block_index + offset) * count + jnp.arange(count, dtype=jnp.int32)[None, :]
        keep = (jnp.abs(row_pos - columns) >= limit) & (block_index + offset < blocks)
        return jnp.where(keep, 1.0 - total, CEILING)

    row_pos = block_index * count + jnp.arange(count, dtype=jnp.int32)[:, None]

    def summed(right, offset):
        total = lax.psum(correlate(query, right), "chan")
        return scored(total, row_pos, offset)

    own_scores = summed(query, 0)
    near_scores = summed(nearby, 1)
    far_scores = summed(faraway, 2)
    row_best = jnp.minimum(
        jnp.min(own_scores, axis=1),
        jnp.minimum(jnp.min(near_scores, axis=1), jnp.min(far_scores, axis=1)),
    )
    near_cols = jnp.min(near_scores, axis=0)
    far_cols = jnp.min(far_scores, axis=0)
    near_home = from_behind(CEILING - near_cols, "tm", 1)
    far_home = from_behind(CEILING - far_cols, "tm", 2)
    return jnp.minimum(row_best, jnp.minimum(CEILING - near_home, CEILING - far_home))


def solution(mesh):
    placed = (P("chan", "tm"), P("chan", None), P())
    return jax.shard_map(on_device, mesh=mesh, in_specs=placed, out_specs=P("tm"), check_vma=False)
```

profile of v0, /device:TPU:9, one launch (start us, length us, event | category | flops | bytes accessed | tf_op | source)
XLA Modules:
  0.0 510.5 jit_solution(10372994987045576951)
XLA Ops:
  6.5 0.0 all-reduce.3.cloned.1.call-start
  6.5 0.7 slice.3
  7.3 2.6 collective-permute-start
  9.9 0.1 copy.27
  10.0 2.3 collective-permute-done
  12.3 0.8 pad_maximum_fusion
  13.2 0.2 copy.18
  13.4 215.5 %gather_fusion = f32[65536,32]{1,0:T(8,128)} fusion(f32[32,639]{0,1:T(8,128)S(1)} %copy.18, s32[65536]{0:T(1024)S(1)} %broadcast_clamp_fusion), kind=kCustom, calls=%fused_computation | custom fusion | bytes 17039360 | tf_op jit(solution)/shard_map/gather | solution.py:22
  228.9 22.1 %copy.26 = f32[128,512,32]{1,0,2:T(8,128)} copy(f32[128,512,32]{2,1,0:T(8,128)} %bitcast.26) | data formatting | bytes 16777216 | tf_op jit(solution)/shard_map/gather | solution.py:22
  251.0 0.0 copy-start
  251.0 4.7 bitcast_reduce_fusion
  255.7 1.0 copy-done
  256.7 1.4 multiply_reduce_fusion
  258.2 1.7 multiply_convert_fusion
  259.9 1.9 collective-permute-start.1
  261.8 4.0 collective-permute-start.2
  265.9 3.4 convolution_bitcast_fusion.2
  269.3 83.4 %collective-permute-done.1 = bf16[32,128,512]{2,1,0:T(8,128)(2,1)S(1)} collective-permute-done((bf16[32,128,512]{2,1,0:T(8,128)(2,1)S(1)}, bf16[32,128,512]{2,1,0:T(8,128)(2,1)S(1)}, u32[]{:S(2)}, u32[]{:S(2)}) %collective-permute-start.1) | collective-permute-done | bytes 4194336 | tf_op jit(solution)/shard_map/ppermute | solution.py:15
  352.7 3.4 convolution_bitcast_fusion.1
  356.1 0.9 collective-permute-done.2
  356.9 3.4 convolution_bitcast_fusion
  360.3 0.0 all-reduce.3.cloned.1.call-update
  361.0 129.8 %all-reduce.3.cloned.1.call-done = (f32[512,512]{1,0:T(8,128)}, f32[512,512]{1,0:T(8,128)}, f32[512,512]{1,0:T(8,128)}) async-done(((f32[512,512]{1,0:T(8,128)}, f32[512,512]{1,0:T(8,128)}, f32[512,512]{1,0:T(8,128)}), (f32[512,512]{1,0:T(8,128)}, f32[512,512]{1,0:T(8,128)}, f32[512,512]{1,0:T(8,128)})) %all-reduce.3.cloned.1.call-update) | async-done | bytes 3145744 | tf_op jit(solution)/shard_map/psum | solution.py:58
  490.8 3.2 fusion.6
  494.0 3.8 collective-permute-start.3
  497.8 3.1 collective-permute-start.4
  500.9 0.0 collective-permute-done.3
  500.9 2.1 collective-permute-done.4
  503.0 0.6 minimum_minimum_fusion
  (9 shorter events, 0.1 us)
Async XLA Ops:
  6.5 484.2 %all-reduce.3.cloned.1.call-start = ((), (), s32[]{:S(2)}) async-start(), calls=%async_computation | async-start | bytes 6291456 | tf_op jit(solution)/shard_map/psum | solution.py:58
  7.3 5.1 collective-permute-start
  251.0 5.8 %copy-start = (f32[128,512,32]{1,0,2:T(8,128)S(1)}, f32[128,512,32]{1,0,2:T(8,128)}, u32[]{:S(2)}) copy-start(f32[128,512,32]{1,0,2:T(8,128)} %copy.26) | copy-start | bytes 25165828
  259.9 92.8 %collective-permute-start.1 = (bf16[32,128,512]{2,1,0:T(8,128)(2,1)S(1)}, bf16[32,128,512]{2,1,0:T(8,128)(2,1)S(1)}, u32[]{:S(2)}, u32[]{:S(2)}) collective-permute-start(bf16[32,128,512]{2,1,0:T(8,128)(2,1)S(1)} %multiply_convert_fusion), channel_id=1, source_target_pairs={{2,0},{4,2},{6,4},{8,6},{10,8},{12,10},{14,12},{16,14},{18,16},{20... | collective-permute-start | bytes 12582920 | tf_op jit(solution)/shard_map/ppermute | solution.py:15
  261.8 95.1 %collective-permute-start.2 = (bf16[32,128,512]{2,1,0:T(8,128)(2,1)S(1)}, bf16[32,128,512]{2,1,0:T(8,128)(2,1)S(1)}, u32[]{:S(2)}, u32[]{:S(2)}) collective-permute-start(bf16[32,128,512]{2,1,0:T(8,128)(2,1)S(1)} %multiply_convert_fusion), channel_id=1, source_target_pairs={{4,0},{6,2},{8,4},{10,6},{12,8},{14,10},{16,12},{18,14},{20,16},{2... | collective-permute-start | bytes 12582920 | tf_op jit(solution)/shard_map/ppermute | solution.py:15
  494.0 7.0 %collective-permute-start.3 = (f32[512]{0:T(512)S(1)}, f32[512]{0:T(512)S(1)}, u32[]{:S(2)}, u32[]{:S(2)}) collective-permute-start(f32[512]{0:T(512)S(1)} %broadcast_subtract_fusion.1), channel_id=1, source_target_pairs={{0,2},{2,4},{4,6},{6,8},{8,10},{10,12},{12,14},{14,16},{16,18},{18... | collective-permute-start | bytes 6152 | tf_op jit(solution)/shard_map/ppermute | solution.py:15
  497.8 5.2 %collective-permute-start.4 = (f32[512]{0:T(512)S(1)}, f32[512]{0:T(512)S(1)}, u32[]{:S(2)}, u32[]{:S(2)}) collective-permute-start(f32[512]{0:T(512)S(1)} %broadcast_subtract_fusion), channel_id=1, source_target_pairs={{0,4},{2,6},{4,8},{6,10},{8,12},{10,14},{12,16},{14,18},{16,20},{1... | collective-permute-start | bytes 6152 | tf_op jit(solution)/shard_map/ppermute | solution.py:15
Sparse Core Ops, SparseCore 0:
  360.4 130.2 all-reduce.2
where the time goes:
time: 511 us; the launch traced here: 510 us
  local copies, waits for them, and re-layouts  240 us (47%)
  waiting for transfers between devices  219 us (43%)
  starting transfers between devices  15.5 us (3%)
  between operations  14.2 us (3%)
  other arithmetic  12.6 us (2%)
  matrix products  10.1 us (2%)
    gather x2, local copies, waits for them, and re-layouts, normalize(): windows = extended[:, starts]  238 us
    psum x1, waiting for transfers between devices, summed(): total = lax.psum(correlate(query, right), 'chan')  130 us
    ppermute x5, waiting for transfers between devices, from_behind(): return lax.ppermute(shard, axis, pairs)  88.8 us
    ppermute x5, starting transfers between devices, from_behind(): return lax.ppermute(shard, axis, pairs)  15.5 us
  transfers between devices with their start and end apart: 6, of which 5 were waited for; matrix products, arithmetic and copies ran while one was open for 1% of the time, Pallas kernels for 0%

commit v1 on v0

--- a/solution.py
+++ b/solution.py
@@ -55,7 +55,9 @@
     row_pos = block_index * count + jnp.arange(count, dtype=jnp.int32)[:, None]
 
     def summed(right, offset):
-        total = lax.psum(correlate(query, right), "chan")
+        part = correlate(query, right)
+        parts = lax.all_gather(part, "chan")
+        total = jnp.sum(parts, axis=0)
         return scored(total, row_pos, offset)
 
     own_scores = summed(query, 0)

time: 511 us -> 464 us (0.908)
  waiting for transfers between devices: 219 us -> 155 us
  matrix products: 10.1 us -> 20.4 us
  other arithmetic: 12.6 us -> 18.6 us
    psum x1 -> x0, waiting for transfers between devices: 130 us -> none  [summed(): total = lax.psum(correlate(query, right), 'chan')]
    all_gather x0 -> x3, waiting for transfers between devices: none -> 70.2 us  [summed(): parts = lax.all_gather(part, 'chan')]
    dot_general x3, matrix products: 10.1 us -> 20.4 us  [correlate(): lax.dot_general(left, right, (((0, 1), (0, 1)), ((), ())), preferred_elem...]
    reduce_sum x0 -> x3, other arithmetic: none -> 5.87 us  [summed(): total = jnp.sum(parts, axis=0)]
  transfers between devices with their start and end apart: 6 -> 8, of which waited for: 5 -> 5; matrix products, arithmetic and copies ran while one was open for 1% -> 5% of each run, Pallas kernels for 0% -> 0%
where the time goes in v1:
time: 464 us; the launch traced here: 463 us
  local copies, waits for them, and re-layouts  240 us (52%)
  waiting for transfers between devices  155 us (33%)
  matrix products  20.4 us (4%)
  other arithmetic  18.6 us (4%)
  starting transfers between devices  15.5 us (3%)
  between operations  13.9 us (3%)
    gather x2, local copies, waits for them, and re-layouts, normalize(): windows = extended[:, starts]  238 us
    ppermute x5, waiting for transfers between devices, from_behind(): return lax.ppermute(shard, axis, pairs)  84.9 us
    all_gather x3, waiting for transfers between devices, summed(): parts = lax.all_gather(part, 'chan')  70.2 us
    dot_general x3, matrix products, correlate(): lax.dot_general(left, right, (((0, 1), (0, 1)), ((), ())), preferred_elem...  20.4 us
    ppermute x5, starting transfers between devices, from_behind(): return lax.ppermute(shard, axis, pairs)  15.3 us
  transfers between devices with their start and end apart: 8, of which 5 were waited for; matrix products, arithmetic and copies ran while one was open for 5% of the time, Pallas kernels for 0%

profile of v1, /device:TPU:9, one launch (start us, length us, event | category | flops | bytes accessed | tf_op | source)
XLA Modules:
  0.0 463.1 jit_solution(14838472900545766581)
XLA Ops:
  6.5 0.0 all-gather.7.cloned.1.call-start
  6.5 0.7 slice.3
  7.3 2.6 collective-permute-start
  9.9 0.1 copy.32
  10.0 2.3 collective-permute-done
  12.3 0.8 pad_maximum_fusion
  13.2 0.2 copy.23
  13.4 215.5 %gather_fusion = f32[65536,32]{1,0:T(8,128)} fusion(f32[32,639]{0,1:T(8,128)S(1)} %copy.23, s32[65536]{0:T(1024)S(1)} %broadcast_clamp_fusion), kind=kCustom, calls=%fused_computation | custom fusion | bytes 17039360 | tf_op jit(solution)/shard_map/gather | solution.py:22
  228.9 22.1 %copy.31 = f32[128,512,32]{1,0,2:T(8,128)} copy(f32[128,512,32]{2,1,0:T(8,128)} %bitcast.29) | data formatting | bytes 16777216 | tf_op jit(solution)/shard_map/gather | solution.py:22
  251.0 0.0 copy-start
  251.0 4.7 %bitcast_reduce_fusion = f32[32,512]{1,0:T(8,128)S(1)} fusion(f32[128,512,32]{1,0,2:T(8,128)} %copy.31), kind=kLoop, calls=%fused_computation.1 | loop fusion | flops 2080768 | bytes 8454144 | tf_op jit(solution)/shard_map/reduce_sum | solution.py:23
  255.7 1.0 copy-done
  256.7 1.4 multiply_reduce_fusion
  258.2 3.6 multiply_convert_fusion
  261.9 1.9 collective-permute-start.1
  263.8 3.9 collective-permute-start.2
  267.6 6.8 %convolution_bitcast_fusion.2 = f32[512,512]{1,0:T(8,128)} fusion(bf16[32,128,512]{2,1,0:T(8,128)(2,1)} %multiply_convert_fusion), kind=kOutput, calls=%fused_computation.7 | convolution fusion | flops 2147483648 | bytes 5242880 | tf_op jit(solution)/shard_map/dot_general | solution.py:31
  274.5 0.0 all-gather.7.cloned.1.call-update
  274.5 0.0 all-gather.9.cloned.1.call-start
  274.5 80.4 %collective-permute-done.1 = bf16[32,128,512]{2,1,0:T(8,128)(2,1)} collective-permute-done((bf16[32,128,512]{2,1,0:T(8,128)(2,1)}, bf16[32,128,512]{2,1,0:T(8,128)(2,1)}, u32[]{:S(2)}, u32[]{:S(2)}) %collective-permute-start.1) | collective-permute-done | bytes 4194336 | tf_op jit(solution)/shard_map/ppermute | solution.py:15
  354.9 6.8 %convolution_bitcast_fusion.1 = f32[512,512]{1,0:T(8,128)} fusion(bf16[32,128,512]{2,1,0:T(8,128)(2,1)} %multiply_convert_fusion, bf16[32,128,512]{2,1,0:T(8,128)(2,1)} %collective-permute-done.1), kind=kOutput, calls=%fused_computation.6 | convolution fusion | flops 2147483648 | bytes 9437184 | tf_op jit(solution)/shard_map/dot_general | solution.py:31
  361.7 0.0 all-gather.9.cloned.1.call-update
  361.8 0.2 all-gather.11.cloned.1.call-start
  362.0 0.0 collective-permute-done.2
  362.0 6.8 %convolution_bitcast_fusion = f32[512,512]{1,0:T(8,128)} fusion(bf16[32,128,512]{2,1,0:T(8,128)(2,1)} %multiply_convert_fusion, bf16[32,128,512]{2,1,0:T(8,128)(2,1)} %collective-permute-done.2), kind=kOutput, calls=%fused_computation.5 | convolution fusion | flops 2147483648 | bytes 9437184 | tf_op jit(solution)/shard_map/dot_general | solution.py:31
  368.8 0.0 all-gather.11.cloned.1.call-update
  369.5 0.0 all-gather.7.cloned.1.call-done
  369.6 2.1 reduce_sum.47
  371.6 25.2 %all-gather.9.cloned.1.call-done = f32[1024,512]{1,0:T(8,128)} async-done(((f32[512,512]{1,0:T(8,128)}), f32[1024,512]{1,0:T(8,128)}) %all-gather.9.cloned.1.call-update) | async-done | bytes 2097168 | tf_op jit(solution)/shard_map/all_gather | solution.py:59
  396.9 1.9 reduce_sum.48
  398.8 44.9 %all-gather.11.cloned.1.call-done = f32[1024,512]{1,0:T(8,128)} async-done(((f32[512,512]{1,0:T(8,128)}), f32[1024,512]{1,0:T(8,128)}) %all-gather.11.cloned.1.call-update) | async-done | bytes 2097168 | tf_op jit(solution)/shard_map/all_gather | solution.py:59
  443.7 1.9 reduce_sum.49
  445.6 1.3 fusion.6
  446.9 3.8 collective-permute-start.3
  450.8 3.1 collective-permute-start.4
  453.9 0.0 collective-permute-done.3
  453.9 2.1 collective-permute-done.4
  456.0 0.6 minimum_minimum_fusion
  (9 shorter events, 0.1 us)
Async XLA Ops:
  6.5 363.0 %all-gather.7.cloned.1.call-start = ((), (), s32[]{:S(2)}) async-start(), calls=%async_computation | async-start | bytes 3145728 | tf_op jit(solution)/shard_map/all_gather | solution.py:59
  7.3 5.1 %collective-permute-start = (f32[32,127]{1,0:T(8,128)S(1)}, f32[32,127]{1,0:T(8,128)S(1)}, u32[]{:S(2)}, u32[]{:S(2)}) collective-permute-start(f32[32,127]{1,0:T(8,128)S(1)} %slice.3), channel_id=1, source_target_pairs={{2,0},{4,2},{6,4},{8,6},{10,8},{12,10},{14,12},{16,14},{18,16},{20... | collective-permute-start | bytes 48776 | tf_op jit(solution)/shard_map/ppermute | solution.py:15
  251.0 5.8 %copy-start = (f32[128,512,32]{1,0,2:T(8,128)S(1)}, f32[128,512,32]{1,0,2:T(8,128)}, u32[]{:S(2)}) copy-start(f32[128,512,32]{1,0,2:T(8,128)} %copy.31) | copy-start | bytes 25165828
  261.9 93.1 %collective-permute-start.1 = (bf16[32,128,512]{2,1,0:T(8,128)(2,1)}, bf16[32,128,512]{2,1,0:T(8,128)(2,1)}, u32[]{:S(2)}, u32[]{:S(2)}) collective-permute-start(bf16[32,128,512]{2,1,0:T(8,128)(2,1)} %multiply_convert_fusion), channel_id=1, source_target_pairs={{2,0},{4,2},{6,4},{8,6},{10,8},{12,10},{14,12},{16,14},{18,16},{20... | collective-permute-start | bytes 12582920 | tf_op jit(solution)/shard_map/ppermute | solution.py:15
  263.8 98.2 %collective-permute-start.2 = (bf16[32,128,512]{2,1,0:T(8,128)(2,1)}, bf16[32,128,512]{2,1,0:T(8,128)(2,1)}, u32[]{:S(2)}, u32[]{:S(2)}) collective-permute-start(bf16[32,128,512]{2,1,0:T(8,128)(2,1)} %multiply_convert_fusion), channel_id=1, source_target_pairs={{4,0},{6,2},{8,4},{10,6},{12,8},{14,10},{16,12},{18,14},{20,16},{2... | collective-permute-start | bytes 12582920 | tf_op jit(solution)/shard_map/ppermute | solution.py:15
  274.5 122.4 %all-gather.9.cloned.1.call-start = ((), (), s32[]{:S(2)}) async-start(), calls=%async_computation.1 | async-start | bytes 3145728 | tf_op jit(solution)/shard_map/all_gather | solution.py:59
  361.8 81.9 %all-gather.11.cloned.1.call-start = ((), (), s32[]{:S(2)}) async-start(), calls=%async_computation.2 | async-start | bytes 3145728 | tf_op jit(solution)/shard_map/all_gather | solution.py:59
  446.9 7.0 %collective-permute-start.3 = (f32[512]{0:T(512)S(1)}, f32[512]{0:T(512)S(1)}, u32[]{:S(2)}, u32[]{:S(2)}) collective-permute-start(f32[512]{0:T(512)S(1)} %broadcast_subtract_fusion.1), channel_id=1, source_target_pairs={{0,2},{2,4},{4,6},{6,8},{8,10},{10,12},{12,14},{14,16},{16,18},{18... | collective-permute-start | bytes 6152 | tf_op jit(solution)/shard_map/ppermute | solution.py:15
  450.8 5.2 %collective-permute-start.4 = (f32[512]{0:T(512)S(1)}, f32[512]{0:T(512)S(1)}, u32[]{:S(2)}, u32[]{:S(2)}) collective-permute-start(f32[512]{0:T(512)S(1)} %broadcast_subtract_fusion), channel_id=1, source_target_pairs={{0,4},{2,6},{4,8},{6,10},{8,12},{10,14},{12,16},{14,18},{16,20},{1... | collective-permute-start | bytes 6152 | tf_op jit(solution)/shard_map/ppermute | solution.py:15
Sparse Core Ops, SparseCore 0:
  274.6 36.2 all-gather.6
  361.9 34.9 all-gather.8
  398.4 45.2 all-gather.10
